TPU v7x, 32 devices: a whole 2x2x4 slice. The times are simulated.
32 devices in a mesh: outer: 4 (over y, x), inner: 8 (over z, core).
Axes of the slice: x: 2, y: 2, z: 4, core: 2. Of those that a mesh axis runs over, the one named last changes fastest.
Arguments:
- queries: bfloat16 [4096, 4096], P(('outer', 'inner')), may hold values from -24 to 24, as said below
- keys: bfloat16 [4096, 1024], P(('outer', 'inner')), may hold values from -24 to 24, as said below
- values: bfloat16 [4096, 1024], P(('outer', 'inner')), may hold values from -6 to 6
Outputs:
- attended: bfloat16 [4096, 4096], P(('outer', 'inner'))
Inputs may be any that keep to these rules, and one draw needn't show every extreme that they name: `queries`: entries of order one, a few larger. `keys`: entries of order one, a few larger.
All inputs are finite; a program needn't handle non-finite values.
Results may differ from a plain program's by a relative error of at most 0.008.
Values may be sent and summed in bfloat16 or wider, within the bound.
No kernel may reach another device: no remote copies, remote signals or barrier semaphores. Data moves between devices by JAX's collectives and lax.ppermute only.
A program may use at most 128 MiB of HBM per device.

v0:
```python
import jax
import jax.numpy as jnp
from jax import lax
from jax.sharding import PartitionSpec as P

QH = 32
KVH = 8
HD = 128


def shifted(block, axis, distance):
    devices = range(lax.axis_size(axis))
    route = [(i - distance, i) for i in devices if i - distance in devices]
    return lax.ppermute(block, axis, route)


def attend(state, near_keys, near_values, allowed, grouped):
    rows = near_keys.shape[0]
    heads = near_keys.shape[1]
    size = 256
    count = rows // size
    scale = 1.0 / HD**0.5
    key_blocks = near_keys.reshape(count, size, heads, HD)
    value_blocks = near_values.reshape(count, size, heads, HD)

    def one_block(carry, pieces):
        peak, total, accum = carry
        key_block, value_block = pieces
        scores = (
            jnp.einsum("qgrd,kgd->grqk", grouped, key_block, preferred_element_type=jnp.float32)
            * scale
        )
        scores = jnp.where(allowed, scores, -jnp.inf)
        upper = jnp.maximum(peak, jnp.max(scores, axis=-1))
        factor = jnp.exp(peak - upper)
        weights = jnp.exp(scores - upper[..., None])
        total = total * factor + jnp.sum(weights, axis=-1)
        update = jnp.einsum(
            "grqk,kgd->grqd",
            weights.astype(jnp.bfloat16),
            value_block,
            preferred_element_type=jnp.float32,
        )
        accum = accum * factor[..., None] + update
        return ((upper, total, accum), None)

    state, unused = lax.scan(one_block, state, (key_blocks, value_blocks))
    return state


def fresh_state(heads, ratio, tokens):
    return (
        jnp.full((heads, ratio, tokens), -jnp.inf, jnp.float32),
        jnp.zeros((heads, ratio, tokens), jnp.float32),
        jnp.zeros((heads, ratio, tokens, HD), jnp.float32),
    )


def shards(queries, keys, values):
    tokens = queries.shape[0]
    position = lax.axis_index("outer")
    before_ok = position > 0
    after_ok = position < lax.axis_size("outer") - 1
    members = lax.axis_size("inner")
    per_device = QH // members
    repeat = members // KVH
    query_heads = queries.reshape(tokens, QH, HD)
    key_heads = jnp.repeat(keys.reshape(tokens, KVH, HD), repeat, axis=1)
    value_heads = jnp.repeat(values.reshape(tokens, KVH, HD), repeat, axis=1)
    group_q, group_k, group_v = (
        lax.all_to_all(query_heads, "inner", split_axis=1, concat_axis=0, tiled=True),
        lax.all_to_all(key_heads, "inner", split_axis=1, concat_axis=0, tiled=True),
        lax.all_to_all(value_heads, "inner", split_axis=1, concat_axis=0, tiled=True),
    )
    rows = group_q.shape[0]
    grouped = group_q.reshape(rows, 1, per_device, HD)
    state = attend(fresh_state(1, per_device, rows), group_k, group_v, True, grouped)
    early_k, early_v = shifted((group_k, group_v), "outer", 1)
    state = attend(state, early_k, early_v, before_ok, grouped)
    late_k, late_v = shifted((group_k, group_v), "outer", -1)
    state = attend(state, late_k, late_v, after_ok, grouped)
    peak, total, accum = state
    mixed = (accum / total[..., None]).astype(jnp.bfloat16)
    mixed = mixed.reshape(per_device, rows, HD).transpose(1, 0, 2)
    back = lax.all_to_all(mixed, "inner", split_axis=0, concat_axis=1, tiled=True)
    return back.reshape(tokens, QH * HD)


def solution(mesh):
    placed = (P(("outer", "inner"), None), P(("outer", "inner"), None), P(("outer", "inner"), None))
    return jax.shard_map(
        shards, mesh=mesh, in_specs=placed, out_specs=P(("outer", "inner"), None), check_vma=False
    )
```

profile of v0, /device:TPU:0, one launch (start us, length us, event | category | flops | bytes accessed | tf_op | source)
XLA Modules:
  0.0 174.7 jit_solution(10812905736298252282)
XLA Ops:
  1.7 6.4 %all-to-all-start = ((bf16[128,8,128]{2,0,1:T(8,128)(2,1)}), bf16[128,8,128]{2,0,1:T(8,128)(2,1)S(1)}, u32[]{:S(2)}, u32[]{:S(2)}) async-start(bf16[128,8,128]{2,0,1:T(8,128)(2,1)} %copy_bitcast_fusion.1), calls=%async_computation | async-start | bytes 524288 | tf_op jit(solution)/shard_map/all_to_all | solution.py:72
  8.1 1.7 copy_bitcast_fusion
  9.8 8.0 %all-to-all-done = bf16[128,8,128]{2,0,1:T(8,128)(2,1)S(1)} async-done(((bf16[128,8,128]{2,0,1:T(8,128)(2,1)}), bf16[128,8,128]{2,0,1:T(8,128)(2,1)S(1)}, u32[]{:S(2)}, u32[]{:S(2)}) %all-to-all-start) | async-done | bytes 262176 | tf_op jit(solution)/shard_map/all_to_all | solution.py:72
  17.8 3.4 %all-to-all-start.2 = ((bf16[128,8,128]{2,0,1:T(8,128)(2,1)}), bf16[128,8,128]{2,0,1:T(8,128)(2,1)S(1)}, u32[]{:S(2)}, u32[]{:S(2)}) async-start(bf16[128,8,128]{2,0,1:T(8,128)(2,1)} %copy_bitcast_fusion), calls=%async_computation.2 | async-start | bytes 524288 | tf_op jit(solution)/shard_map/all_to_all | solution.py:73
  21.2 2.3 %copy.29 = bf16[128,4096]{0,1:T(8,128)(2,1)} copy(bf16[128,4096]{1,0:T(8,128)(2,1)} %param.9) | data formatting | bytes 2097152 | tf_op args[0]
  23.5 7.4 %all-to-all-done.2 = bf16[128,8,128]{2,0,1:T(8,128)(2,1)S(1)} async-done(((bf16[128,8,128]{2,0,1:T(8,128)(2,1)}), bf16[128,8,128]{2,0,1:T(8,128)(2,1)S(1)}, u32[]{:S(2)}, u32[]{:S(2)}) %all-to-all-start.2) | async-done | bytes 262176 | tf_op jit(solution)/shard_map/all_to_all | solution.py:73
  31.5 3.6 %all-to-all-start.1 = ((bf16[128,32,128]{0,2,1:T(8,128)(2,1)}), bf16[128,32,128]{0,2,1:T(8,128)(2,1)S(1)}, u32[]{:S(2)}, u32[]{:S(2)}) async-start(bf16[128,32,128]{0,2,1:T(8,128)(2,1)} %bitcast.31), calls=%async_computation.1 | async-start | bytes 2097152 | tf_op jit(solution)/shard_map/all_to_all | solution.py:71
  35.1 4.1 %collective-permute-start = (bf16[1024,1,128]{2,0,1:T(8,128)(2,1)}, bf16[1024,1,128]{2,0,1:T(8,128)(2,1)}, u32[]{:S(2)}, u32[]{:S(2)}) collective-permute-start(bf16[1024,1,128]{2,0,1:T(8,128)(2,1)} %bitcast.261), channel_id=1, source_target_pairs={{0,8},{8,16},{16,24},{1,9},{9,17},{17,25},{2,10},{10,18},{18,26},{... | collective-permute-start | bytes 786440 | tf_op jit(solution)/shard_map/ppermute | solution.py:14
  40.5 5.3 %collective-permute-start.1 = (bf16[1024,1,128]{2,0,1:T(8,128)(2,1)}, bf16[1024,1,128]{2,0,1:T(8,128)(2,1)}, u32[]{:S(2)}, u32[]{:S(2)}) collective-permute-start(bf16[1024,1,128]{2,0,1:T(8,128)(2,1)} %bitcast.264), channel_id=1, source_target_pairs={{0,8},{8,16},{16,24},{1,9},{9,17},{17,25},{2,10},{10,18},{18,26},{... | collective-permute-start | bytes 786440 | tf_op jit(solution)/shard_map/ppermute | solution.py:14
  47.1 14.5 %all-to-all-done.1 = bf16[128,32,128]{0,2,1:T(8,128)(2,1)S(1)} async-done(((bf16[128,32,128]{0,2,1:T(8,128)(2,1)}), bf16[128,32,128]{0,2,1:T(8,128)(2,1)S(1)}, u32[]{:S(2)}, u32[]{:S(2)}) %all-to-all-start.1) | async-done | bytes 1048608 | tf_op jit(solution)/shard_map/all_to_all | solution.py:71
  62.6 1.6 copy.31
  64.2 31.1 %while.45 = (s32[]{:T(128)}, f32[1,4,1024]{2,1,0:T(4,128)S(1)}, f32[1,4,1024]{2,1,0:T(4,128)S(1)}, f32[1,4,1024,128]{3,2,1,0:T(8,128)S(1)}, bf16[4,256,1,128]{3,...) while((s32[]{:T(128)}, f32[1,4,1024]{2,1,0:T(4,128)S(1)}, ...), condition=%wide.region_3.4_spmd.clone, body=%wide.region_0.3_spmd.clone.sunk | while | flops 546856960 | bytes 34997380 | solution.py:47
  64.2 3.5 %bitcast_reduce_fusion.8 = (f32[4,1024]{1,0:T(4,128)S(1)}, f32[256,1024,4]{1,0,2:T(8,128)}) fusion(bf16[1024,1,4,128]{3,0,2,1:T(8,128)(2,1)S(1)} %get-tuple-element.409, bf16[4,256,1,128]{3,1,2,0:T(8,128)(2,1)} %get-tuple-element.408, s32[]{:T(128)} %get-tuple-element.395), kind=kOutput, calls=%fused_computation.55.clone.1 | convolution fusion | flops 270528512 | bytes 5325312 | tf_op jit(solution)/shard_map/while/body/eval_jaxpr/qgrd,kgd->grqk/dot_general | solution.py:30
  67.7 3.3 %bitcast_add_fusion.17 = f32[1,4,1024,128]{3,2,1,0:T(8,128)S(1)} fusion(f32[1,4,1024,128]{3,2,1,0:T(8,128)S(1)} %get-tuple-element.398, f32[256,1024,4]{1,0,2:T(8,128)} %get-tuple-element.384, f32[4,1024]{1,0:T(4,128)S(1)} %bitcast.252, f32[4,1024]{1,0:T(4,128)S(1)} %get-tuple-element.385, pred[]{:T(512)S(6)} %compare.3, ...), kind=kOutput, calls=%fused_computation.61.clone.1 | convolution fusion | flops 273154048 | bytes 8487425 | tf_op jit(solution)/shard_map/while/body/eval_jaxpr/grqk,kgd->grqd/dot_general | solution.py:38
  72.0 3.5 %bitcast_reduce_fusion.8 = (f32[4,1024]{1,0:T(4,128)S(1)}, f32[256,1024,4]{1,0,2:T(8,128)}) fusion(bf16[1024,1,4,128]{3,0,2,1:T(8,128)(2,1)S(1)} %get-tuple-element.409, bf16[4,256,1,128]{3,1,2,0:T(8,128)(2,1)} %get-tuple-element.408, s32[]{:T(128)} %get-tuple-element.395), kind=kOutput, calls=%fused_computation.55.clone.1 | convolution fusion | flops 270528512 | bytes 5325312 | tf_op jit(solution)/shard_map/while/body/eval_jaxpr/qgrd,kgd->grqk/dot_general | solution.py:30
  75.5 3.3 %bitcast_add_fusion.17 = f32[1,4,1024,128]{3,2,1,0:T(8,128)S(1)} fusion(f32[1,4,1024,128]{3,2,1,0:T(8,128)S(1)} %get-tuple-element.398, f32[256,1024,4]{1,0,2:T(8,128)} %get-tuple-element.384, f32[4,1024]{1,0:T(4,128)S(1)} %bitcast.252, f32[4,1024]{1,0:T(4,128)S(1)} %get-tuple-element.385, pred[]{:T(512)S(6)} %compare.3, ...), kind=kOutput, calls=%fused_computation.61.clone.1 | convolution fusion | flops 273154048 | bytes 8487425 | tf_op jit(solution)/shard_map/while/body/eval_jaxpr/grqk,kgd->grqd/dot_general | solution.py:38
  79.7 3.5 %bitcast_reduce_fusion.8 = (f32[4,1024]{1,0:T(4,128)S(1)}, f32[256,1024,4]{1,0,2:T(8,128)}) fusion(bf16[1024,1,4,128]{3,0,2,1:T(8,128)(2,1)S(1)} %get-tuple-element.409, bf16[4,256,1,128]{3,1,2,0:T(8,128)(2,1)} %get-tuple-element.408, s32[]{:T(128)} %get-tuple-element.395), kind=kOutput, calls=%fused_computation.55.clone.1 | convolution fusion | flops 270528512 | bytes 5325312 | tf_op jit(solution)/shard_map/while/body/eval_jaxpr/qgrd,kgd->grqk/dot_general | solution.py:30
  83.3 3.3 %bitcast_add_fusion.17 = f32[1,4,1024,128]{3,2,1,0:T(8,128)S(1)} fusion(f32[1,4,1024,128]{3,2,1,0:T(8,128)S(1)} %get-tuple-element.398, f32[256,1024,4]{1,0,2:T(8,128)} %get-tuple-element.384, f32[4,1024]{1,0:T(4,128)S(1)} %bitcast.252, f32[4,1024]{1,0:T(4,128)S(1)} %get-tuple-element.385, pred[]{:T(512)S(6)} %compare.3, ...), kind=kOutput, calls=%fused_computation.61.clone.1 | convolution fusion | flops 273154048 | bytes 8487425 | tf_op jit(solution)/shard_map/while/body/eval_jaxpr/grqk,kgd->grqd/dot_general | solution.py:38
  87.5 3.5 %bitcast_reduce_fusion.8 = (f32[4,1024]{1,0:T(4,128)S(1)}, f32[256,1024,4]{1,0,2:T(8,128)}) fusion(bf16[1024,1,4,128]{3,0,2,1:T(8,128)(2,1)S(1)} %get-tuple-element.409, bf16[4,256,1,128]{3,1,2,0:T(8,128)(2,1)} %get-tuple-element.408, s32[]{:T(128)} %get-tuple-element.395), kind=kOutput, calls=%fused_computation.55.clone.1 | convolution fusion | flops 270528512 | bytes 5325312 | tf_op jit(solution)/shard_map/while/body/eval_jaxpr/qgrd,kgd->grqk/dot_general | solution.py:30
  91.0 3.3 %bitcast_add_fusion.17 = f32[1,4,1024,128]{3,2,1,0:T(8,128)S(1)} fusion(f32[1,4,1024,128]{3,2,1,0:T(8,128)S(1)} %get-tuple-element.398, f32[256,1024,4]{1,0,2:T(8,128)} %get-tuple-element.384, f32[4,1024]{1,0:T(4,128)S(1)} %bitcast.252, f32[4,1024]{1,0:T(4,128)S(1)} %get-tuple-element.385, pred[]{:T(512)S(6)} %compare.3, ...), kind=kOutput, calls=%fused_computation.61.clone.1 | convolution fusion | flops 273154048 | bytes 8487425 | tf_op jit(solution)/shard_map/while/body/eval_jaxpr/grqk,kgd->grqd/dot_general | solution.py:38
  95.3 20.8 %while.43 = (s32[]{:T(128)}, f32[1,4,1024]{2,1,0:T(4,128)S(1)}, f32[1,4,1024]{2,1,0:T(4,128)S(1)}, f32[1,4,1024,128]{3,2,1,0:T(8,128)S(1)}, pred[]{:T(512)}, /*i...) while((s32[]{:T(128)}, f32[1,4,1024]{2,1,0:T(4,128)S(1)}, ...), condition=%wide.region_7.8_spmd, body=%wide.region_4.7_spmd.sunk | while | flops 549466112 | bytes 18221148 | solution.py:47
  96.9 2.7 %bitcast_add_fusion.13 = f32[1,4,1024,128]{3,2,1,0:T(8,128)S(1)} fusion(f32[1,4,1024,128]{3,2,1,0:T(8,128)S(1)} %get-tuple-element.425, f32[256,1024,4]{1,0,2:T(8,128)S(1)} %get-tuple-element.361, f32[4,1024]{1,0:T(4,128)S(1)} %bitcast.254, pred[]{:T(512)} %get-tuple-element.435, f32[4,1024]{1,0:T(4,128)S(1)} %get-tuple-element.362, ...), kind=kOutput, calls=%fused_computation.8.clone.1 | convolution fusion | flops 273678336 | bytes 8487936 | tf_op jit(solution)/shard_map/while/body/eval_jaxpr/grqk,kgd->grqd/dot_general | solution.py:38
  102.1 2.7 %bitcast_add_fusion.13 = f32[1,4,1024,128]{3,2,1,0:T(8,128)S(1)} fusion(f32[1,4,1024,128]{3,2,1,0:T(8,128)S(1)} %get-tuple-element.425, f32[256,1024,4]{1,0,2:T(8,128)S(1)} %get-tuple-element.361, f32[4,1024]{1,0:T(4,128)S(1)} %bitcast.254, pred[]{:T(512)} %get-tuple-element.435, f32[4,1024]{1,0:T(4,128)S(1)} %get-tuple-element.362, ...), kind=kOutput, calls=%fused_computation.8.clone.1 | convolution fusion | flops 273678336 | bytes 8487936 | tf_op jit(solution)/shard_map/while/body/eval_jaxpr/grqk,kgd->grqd/dot_general | solution.py:38
  107.3 2.7 %bitcast_add_fusion.13 = f32[1,4,1024,128]{3,2,1,0:T(8,128)S(1)} fusion(f32[1,4,1024,128]{3,2,1,0:T(8,128)S(1)} %get-tuple-element.425, f32[256,1024,4]{1,0,2:T(8,128)S(1)} %get-tuple-element.361, f32[4,1024]{1,0:T(4,128)S(1)} %bitcast.254, pred[]{:T(512)} %get-tuple-element.435, f32[4,1024]{1,0:T(4,128)S(1)} %get-tuple-element.362, ...), kind=kOutput, calls=%fused_computation.8.clone.1 | convolution fusion | flops 273678336 | bytes 8487936 | tf_op jit(solution)/shard_map/while/body/eval_jaxpr/grqk,kgd->grqd/dot_general | solution.py:38
  112.5 2.7 %bitcast_add_fusion.13 = f32[1,4,1024,128]{3,2,1,0:T(8,128)S(1)} fusion(f32[1,4,1024,128]{3,2,1,0:T(8,128)S(1)} %get-tuple-element.425, f32[256,1024,4]{1,0,2:T(8,128)S(1)} %get-tuple-element.361, f32[4,1024]{1,0:T(4,128)S(1)} %bitcast.254, pred[]{:T(512)} %get-tuple-element.435, f32[4,1024]{1,0:T(4,128)S(1)} %get-tuple-element.362, ...), kind=kOutput, calls=%fused_computation.8.clone.1 | convolution fusion | flops 273678336 | bytes 8487936 | tf_op jit(solution)/shard_map/while/body/eval_jaxpr/grqk,kgd->grqd/dot_general | solution.py:38
  116.1 20.8 %while.44 = (s32[]{:T(128)}, f32[1,4,1024]{2,1,0:T(4,128)S(1)}, f32[1,4,1024]{2,1,0:T(4,128)S(1)}, f32[1,4,1024,128]{3,2,1,0:T(8,128)S(1)}, pred[]{:T(512)}, /*i...) while((s32[]{:T(128)}, f32[1,4,1024]{2,1,0:T(4,128)S(1)}, ...), condition=%wide.region_11.12_spmd, body=%wide.region_8.11_spmd.sunk | while | flops 549466112 | bytes 18221148 | solution.py:47
  117.7 2.7 %bitcast_add_fusion.15 = f32[1,4,1024,128]{3,2,1,0:T(8,128)S(1)} fusion(f32[1,4,1024,128]{3,2,1,0:T(8,128)S(1)} %get-tuple-element.452, f32[256,1024,4]{1,0,2:T(8,128)S(1)} %get-tuple-element.373, f32[4,1024]{1,0:T(4,128)S(1)} %bitcast.256, pred[]{:T(512)} %get-tuple-element.462, f32[4,1024]{1,0:T(4,128)S(1)} %get-tuple-element.374, ...), kind=kOutput, calls=%fused_computation.35.clone.1 | convolution fusion | flops 273678336 | bytes 8487936 | tf_op jit(solution)/shard_map/while/body/eval_jaxpr/grqk,kgd->grqd/dot_general | solution.py:38
  122.9 2.7 %bitcast_add_fusion.15 = f32[1,4,1024,128]{3,2,1,0:T(8,128)S(1)} fusion(f32[1,4,1024,128]{3,2,1,0:T(8,128)S(1)} %get-tuple-element.452, f32[256,1024,4]{1,0,2:T(8,128)S(1)} %get-tuple-element.373, f32[4,1024]{1,0:T(4,128)S(1)} %bitcast.256, pred[]{:T(512)} %get-tuple-element.462, f32[4,1024]{1,0:T(4,128)S(1)} %get-tuple-element.374, ...), kind=kOutput, calls=%fused_computation.35.clone.1 | convolution fusion | flops 273678336 | bytes 8487936 | tf_op jit(solution)/shard_map/while/body/eval_jaxpr/grqk,kgd->grqd/dot_general | solution.py:38
  128.1 2.7 %bitcast_add_fusion.15 = f32[1,4,1024,128]{3,2,1,0:T(8,128)S(1)} fusion(f32[1,4,1024,128]{3,2,1,0:T(8,128)S(1)} %get-tuple-element.452, f32[256,1024,4]{1,0,2:T(8,128)S(1)} %get-tuple-element.373, f32[4,1024]{1,0:T(4,128)S(1)} %bitcast.256, pred[]{:T(512)} %get-tuple-element.462, f32[4,1024]{1,0:T(4,128)S(1)} %get-tuple-element.374, ...), kind=kOutput, calls=%fused_computation.35.clone.1 | convolution fusion | flops 273678336 | bytes 8487936 | tf_op jit(solution)/shard_map/while/body/eval_jaxpr/grqk,kgd->grqd/dot_general | solution.py:38
  133.3 2.7 %bitcast_add_fusion.15 = f32[1,4,1024,128]{3,2,1,0:T(8,128)S(1)} fusion(f32[1,4,1024,128]{3,2,1,0:T(8,128)S(1)} %get-tuple-element.452, f32[256,1024,4]{1,0,2:T(8,128)S(1)} %get-tuple-element.373, f32[4,1024]{1,0:T(4,128)S(1)} %bitcast.256, pred[]{:T(512)} %get-tuple-element.462, f32[4,1024]{1,0:T(4,128)S(1)} %get-tuple-element.374, ...), kind=kOutput, calls=%fused_computation.35.clone.1 | convolution fusion | flops 273678336 | bytes 8487936 | tf_op jit(solution)/shard_map/while/body/eval_jaxpr/grqk,kgd->grqd/dot_general | solution.py:38
  137.2 6.5 %fusion.67 = bf16[1024,4,128]{2,1,0:T(4,128)(2,1)S(1)} fusion(f32[4,1024]{0,1:T(8,128)S(1)} %copy.33, f32[1,4,1024,128]{3,2,1,0:T(8,128)S(1)} %get-tuple-element.137), kind=kLoop, calls=%fused_computation.81 | loop fusion | flops 1048576 | bytes 3162112 | tf_op jit(solution)/shard_map/transpose | solution.py:84
  143.7 29.0 %all_to_all.66 = bf16[1024,4,128]{2,1,0:T(4,128)(2,1)S(1)} all-to-all(bf16[1024,4,128]{2,1,0:T(4,128)(2,1)S(1)} %fusion.67), channel_id=1, replica_groups=mesh['outer'=4,'inner'=8] {'inner'}, dimensions={0} | all-to-all | bytes 2097152 | tf_op jit(solution)/shard_map/all_to_all | solution.py:85
  (85 shorter events, 31.7 us)
Async XLA Ops:
  0.0 1.0 copy-start
  1.7 16.1 %all-to-all-start = ((bf16[128,8,128]{2,0,1:T(8,128)(2,1)}), bf16[128,8,128]{2,0,1:T(8,128)(2,1)S(1)}, u32[]{:S(2)}, u32[]{:S(2)}) async-start(bf16[128,8,128]{2,0,1:T(8,128)(2,1)} %copy_bitcast_fusion.1), calls=%async_computation | async-start | bytes 524288 | tf_op jit(solution)/shard_map/all_to_all | solution.py:72
  17.8 13.1 %copy-start.3 = (bf16[128,8,128]{2,0,1:T(8,128)(2,1)}, bf16[128,8,128]{2,0,1:T(8,128)(2,1)S(1)}, u32[]{:S(2)}) copy-start(bf16[128,8,128]{2,0,1:T(8,128)(2,1)S(1)} %all-to-all-done) | copy-start | bytes 786436
  17.8 13.1 %all-to-all-start.2 = ((bf16[128,8,128]{2,0,1:T(8,128)(2,1)}), bf16[128,8,128]{2,0,1:T(8,128)(2,1)S(1)}, u32[]{:S(2)}, u32[]{:S(2)}) async-start(bf16[128,8,128]{2,0,1:T(8,128)(2,1)} %copy_bitcast_fusion), calls=%async_computation.2 | async-start | bytes 524288 | tf_op jit(solution)/shard_map/all_to_all | solution.py:73
  30.8 0.7 copy-start.4
  31.5 30.1 %all-to-all-start.1 = ((bf16[128,32,128]{0,2,1:T(8,128)(2,1)}), bf16[128,32,128]{0,2,1:T(8,128)(2,1)S(1)}, u32[]{:S(2)}, u32[]{:S(2)}) async-start(bf16[128,32,128]{0,2,1:T(8,128)(2,1)} %bitcast.31), calls=%async_computation.1 | async-start | bytes 2097152 | tf_op jit(solution)/shard_map/all_to_all | solution.py:71
  35.1 60.1 %collective-permute-start = (bf16[1024,1,128]{2,0,1:T(8,128)(2,1)}, bf16[1024,1,128]{2,0,1:T(8,128)(2,1)}, u32[]{:S(2)}, u32[]{:S(2)}) collective-permute-start(bf16[1024,1,128]{2,0,1:T(8,128)(2,1)} %bitcast.261), channel_id=1, source_target_pairs={{0,8},{8,16},{16,24},{1,9},{9,17},{17,25},{2,10},{10,18},{18,26},{... | collective-permute-start | bytes 786440 | tf_op jit(solution)/shard_map/ppermute | solution.py:14
  39.3 76.8 %collective-permute-start.2 = (bf16[1024,1,128]{2,0,1:T(8,128)(2,1)}, bf16[1024,1,128]{2,0,1:T(8,128)(2,1)}, u32[]{:S(2)}, u32[]{:S(2)}) collective-permute-start(bf16[1024,1,128]{2,0,1:T(8,128)(2,1)} %bitcast.262), channel_id=1, source_target_pairs={{8,0},{16,8},{24,16},{9,1},{17,9},{25,17},{10,2},{18,10},{26,18},{... | collective-permute-start | bytes 786440 | tf_op jit(solution)/shard_map/ppermute | solution.py:14
  40.5 54.7 %collective-permute-start.1 = (bf16[1024,1,128]{2,0,1:T(8,128)(2,1)}, bf16[1024,1,128]{2,0,1:T(8,128)(2,1)}, u32[]{:S(2)}, u32[]{:S(2)}) collective-permute-start(bf16[1024,1,128]{2,0,1:T(8,128)(2,1)} %bitcast.264), channel_id=1, source_target_pairs={{0,8},{8,16},{16,24},{1,9},{9,17},{17,25},{2,10},{10,18},{18,26},{... | collective-permute-start | bytes 786440 | tf_op jit(solution)/shard_map/ppermute | solution.py:14
  45.8 70.3 %collective-permute-start.3 = (bf16[1024,1,128]{2,0,1:T(8,128)(2,1)}, bf16[1024,1,128]{2,0,1:T(8,128)(2,1)}, u32[]{:S(2)}, u32[]{:S(2)}) collective-permute-start(bf16[1024,1,128]{2,0,1:T(8,128)(2,1)} %bitcast.265), channel_id=1, source_target_pairs={{8,0},{16,8},{24,16},{9,1},{17,9},{25,17},{10,2},{18,10},{26,18},{... | collective-permute-start | bytes 786440 | tf_op jit(solution)/shard_map/ppermute | solution.py:14
  61.6 1.0 copy-start.2
  67.7 3.5 %copy-start.1 = (f32[256,1024,4]{1,0,2:T(8,128)S(1)}, f32[256,1024,4]{1,0,2:T(8,128)}, u32[]{:S(2)}) copy-start(f32[256,1024,4]{1,0,2:T(8,128)} %get-tuple-element.384) | copy-start | bytes 12582916 | tf_op jit(solution)/shard_map/while
  75.5 3.5 %copy-start.1 = (f32[256,1024,4]{1,0,2:T(8,128)S(1)}, f32[256,1024,4]{1,0,2:T(8,128)}, u32[]{:S(2)}) copy-start(f32[256,1024,4]{1,0,2:T(8,128)} %get-tuple-element.384) | copy-start | bytes 12582916 | tf_op jit(solution)/shard_map/while
  83.3 3.5 %copy-start.1 = (f32[256,1024,4]{1,0,2:T(8,128)S(1)}, f32[256,1024,4]{1,0,2:T(8,128)}, u32[]{:S(2)}) copy-start(f32[256,1024,4]{1,0,2:T(8,128)} %get-tuple-element.384) | copy-start | bytes 12582916 | tf_op jit(solution)/shard_map/while
  91.0 3.5 %copy-start.1 = (f32[256,1024,4]{1,0,2:T(8,128)S(1)}, f32[256,1024,4]{1,0,2:T(8,128)}, u32[]{:S(2)}) copy-start(f32[256,1024,4]{1,0,2:T(8,128)} %get-tuple-element.384) | copy-start | bytes 12582916 | tf_op jit(solution)/shard_map/while
where the time goes:
time: 176 us; the launch traced here: 175 us
  matrix products  61.1 us (35%)
  waiting for transfers between devices  29.9 us (17%)
  blocking collectives  29 us (16%)
  starting transfers between devices  25.3 us (14%)
  other arithmetic  16.8 us (10%)
  local copies, waits for them, and re-layouts  11.9 us (7%)
    dot_general x12, matrix products, one_block(): jnp.einsum('grqk,kgd->grqd', weights.astype(jnp.bfloat16), value_block, p...  34.6 us
    all_to_all x1, blocking collectives, shards(): lax.all_to_all(mixed, 'inner', split_axis=0, concat_axis=1, tiled=True)  29 us
    dot_general x12, matrix products, one_block(): jnp.einsum('qgrd,kgd->grqk', grouped, key_block, preferred_element_type=j...  26.5 us
    all_to_all x1, waiting for transfers between devices, shards(): lax.all_to_all(query_heads, 'inner', split_axis=1, concat_axis=0, tiled=T...  14.5 us
    ppermute x4, starting transfers between devices, shifted(): return lax.ppermute(block, axis, route)  11.9 us
    reduce_sum x12, other arithmetic, one_block(): total = total * factor + jnp.sum(weights, axis=-1)  9.77 us
    all_to_all x1, waiting for transfers between devices, shards(): lax.all_to_all(key_heads, 'inner', split_axis=1, concat_axis=0, tiled=True)  8.01 us
    all_to_all x1, waiting for transfers between devices, shards(): lax.all_to_all(value_heads, 'inner', split_axis=1, concat_axis=0, tiled=T...  7.37 us
  transfers between devices with their start and end apart: 7, of which 3 were waited for; matrix products, arithmetic and copies ran while one was open for 32% of the time, Pallas kernels for 0%

commit v1 on v0

v1 whole, which is shorter than its diff:
```python
import functools

import jax
import jax.numpy as jnp
from jax import lax
from jax.experimental import pallas as pl
from jax.experimental.pallas import tpu as pltpu
from jax.sharding import PartitionSpec as P

QH = 32
KVH = 8
HD = 128
SPLIT = 4
LOG2E = 1.4426950408889634


def swap(block, axis, bits):
    count = lax.axis_size(axis)
    return lax.ppermute(block, axis, [(i, i ^ bits) for i in range(count)])


def relay(block, axis):
    count = lax.axis_size(axis)
    route = []
    for i in range(count):
        target = i + 2 if i % 2 == 0 else i - 2
        if 0 <= target < count:
            route.append((i, target))
    return lax.ppermute(block, axis, route)


def columns(array, start, width):
    return lax.dynamic_slice_in_dim(array, start, width, 1)


def attend_kernel(first, last, pieces, sources, *refs):
    flag = refs[0]
    q_refs = refs[1 : 1 + sources]
    kv_refs = refs[1 + sources : 1 + sources + pieces]
    at = 1 + sources + pieces
    if not first:
        peak_in, total_in, accum_in = refs[at : at + 3]
        at += 3
    if last:
        out_refs = refs[at : at + sources]
        at += sources
    else:
        peak_out, total_out, accum_out = refs[at : at + 3]
        at += 3
    ratio = QH // KVH
    rows = q_refs[0].shape[0]
    factor = LOG2E / HD**0.5

    def finish(s, accum, total):
        mixed = (accum / total).astype(jnp.bfloat16)
        for r in range(ratio):
            out_refs[s][:, r * HD : (r + 1) * HD] = mixed[r * rows : (r + 1) * rows]

    def compute():
        values = [
            jnp.concatenate([ref[1], jnp.ones_like(ref[1])], axis=1) for ref in kv_refs
        ]
        for s in range(sources):
            q = jnp.concatenate(
                [q_refs[s][:, r * HD : (r + 1) * HD] for r in range(ratio)], axis=0
            )
            scores = [
                lax.dot_general(
                    q, ref[0], (((1,), (1,)), ((), ())), preferred_element_type=jnp.float32
                )
                for ref in kv_refs
            ]
            peak = functools.reduce(
                jnp.maximum, [jnp.max(x, axis=1, keepdims=True) for x in scores]
            )
            if not first:
                old = peak_in[0, s][:, :1]
                peak = jnp.maximum(peak, old)
            update = 0.0
            for x, v in zip(scores, values):
                weights = jnp.exp2((x - peak) * factor).astype(jnp.bfloat16)
                update = update + jnp.dot(weights, v, preferred_element_type=jnp.float32)
            accum, total = update[:, :HD], update[:, HD:]
            if not first:
                shrink = jnp.exp2((old - peak) * factor)
                accum = accum + accum_in[0, s] * shrink
                total = total + total_in[0, s] * shrink
            if last:
                finish(s, accum, total)
            else:
                peak_out[0, s] = jnp.broadcast_to(peak, total.shape)
                total_out[0, s] = total
                accum_out[0, s] = accum

    if first:
        compute()
        return

    pl.when(flag[0] != 0)(compute)

    @pl.when(flag[0] == 0)
    def _():
        for s in range(sources):
            if last:
                finish(s, accum_in[0, s], total_in[0, s])
            else:
                peak_out[0, s] = peak_in[0, s]
                total_out[0, s] = total_in[0, s]
                accum_out[0, s] = accum_in[0, s]


def attend(flag, qs, kvs, state, last):
    ratio = QH // KVH
    sources, pieces = len(qs), len(kvs)
    heads = kvs[0].shape[2] // HD
    rows, width = qs[0].shape
    keys = kvs[0].shape[1]
    first = state is None
    q_spec = pl.BlockSpec((rows, ratio * HD), lambda j, f: (0, j))
    kv_spec = pl.BlockSpec((2, keys, HD), lambda j, f: (0, 0, j))
    state_spec = pl.BlockSpec((1, sources, ratio * rows, HD), lambda j, f: (j, 0, 0, 0))
    state_shape = jax.ShapeDtypeStruct((heads, sources, ratio * rows, HD), jnp.float32)
    in_specs = [q_spec] * sources + [kv_spec] * pieces + ([] if first else [state_spec] * 3)
    if last:
        out_specs = [q_spec] * sources
        out_shape = [jax.ShapeDtypeStruct((rows, width), jnp.bfloat16)] * sources
    else:
        out_specs = [state_spec] * 3
        out_shape = [state_shape] * 3
    total_rows = heads * ratio * rows * sources
    total_keys = pieces * keys
    return pl.pallas_call(
        functools.partial(attend_kernel, first, last, pieces, sources),
        grid_spec=pltpu.PrefetchScalarGridSpec(
            num_scalar_prefetch=1, grid=(heads,), in_specs=in_specs, out_specs=out_specs
        ),
        out_shape=out_shape,
        cost_estimate=pl.CostEstimate(
            flops=4 * total_rows * total_keys * HD,
            transcendentals=total_rows * total_keys,
            bytes_accessed=4 * total_rows * HD * 4,
        ),
        compiler_params=pltpu.CompilerParams(vmem_limit_bytes=40 * 2**20),
        name="attend_last" if last else "attend_first" if first else "attend_next",
    )(flag, *qs, *kvs, *(() if first else state))


def shards(queries, keys, values):
    position = lax.axis_index("outer")
    groups = lax.axis_size("outer")
    members = lax.axis_size("inner")
    me = lax.axis_index("inner")
    core, side = me % 2, me // 2 % 2
    q_width = queries.shape[1] // SPLIT
    kv_width = keys.shape[1] // SPLIT

    def core_part(which):
        parts = [columns(x, which * 2 * kv_width, 2 * kv_width) for x in (keys, values)]
        return jnp.stack(parts)

    kept = core_part(core)
    came = swap(core_part(1 - core), "inner", 1)
    chip = jnp.concatenate([kept, came], axis=1)
    same = lax.dynamic_slice_in_dim(chip, side * kv_width, kv_width, 2)
    other = lax.dynamic_slice_in_dim(chip, (1 - side) * kv_width, kv_width, 2)

    def quarter(which):
        return columns(queries, ((which % 2) * 2 + which // 2 % 2) * q_width, q_width)

    near = [same] + [
        swap(other if hop % 2 else same, "inner", 2 * hop) for hop in range(1, members // 2)
    ]
    qs = [quarter(me)] + [swap(quarter(me ^ bits), "inner", bits) for bits in range(1, SPLIT)]

    side_group = [swap(piece, "outer", 1) for piece in near]
    far_group = [relay(piece, "outer") for piece in side_group]
    far_ok = jnp.where(position % 2 == 0, position > 0, position < groups - 1)
    far_flag = far_ok.astype(jnp.int32).reshape(1)
    always = jnp.ones((1,), jnp.int32)

    state = attend(always, qs, near, None, False)
    state = attend(always, qs, side_group, state, False)
    outs = attend(far_flag, qs, far_group, state, True)
    outs = [outs[0]] + [swap(outs[bits], "inner", bits) for bits in range(1, SPLIT)]

    result = jnp.zeros_like(queries)
    for bits in range(SPLIT):
        which = me ^ bits
        start = ((which % 2) * 2 + which // 2 % 2) * q_width
        result = lax.dynamic_update_slice_in_dim(result, outs[bits], start, 1)
    return result


def solution(mesh):
    placed = P(("outer", "inner"), None)
    return jax.shard_map(
        shards, mesh=mesh, in_specs=(placed, placed, placed), out_specs=placed, check_vma=False
    )
```

time: 176 us -> 84.7 us (0.48)
  the two profiles are of different devices: /device:TPU:0 before, /device:TPU:19 now
where the time goes in v1:
time: 84.7 us; the launch traced here: 84.5 us
  waiting for transfers between devices  39.5 us (47%)
  Pallas kernels  23.6 us (28%)
  starting transfers between devices  16.8 us (20%)
  local copies, waits for them, and re-layouts  4.27 us (5%)
    ppermute x14, waiting for transfers between devices, swap(): return lax.ppermute(block, axis, [(i, i ^ bits) for i in range(count)])  39.5 us
    pallas_call x3, Pallas kernels, attend(): pl.pallas_call(functools.partial(attend_kernel, first, last, pieces, sour...  23.6 us
    ppermute x14, starting transfers between devices, swap(): return lax.ppermute(block, axis, [(i, i ^ bits) for i in range(count)])  11.7 us
    ppermute x4, starting transfers between devices, relay(): return lax.ppermute(block, axis, route)  5.13 us
  transfers between devices with their start and end apart: 18, of which 7 were waited for; matrix products, arithmetic and copies ran while one was open for 1% of the time, Pallas kernels for 19%

profile of v1, /device:TPU:19, one launch (start us, length us, event | category | flops | bytes accessed | tf_op | source)
XLA Modules:
  0.0 84.5 jit_solution(1976257628688412114)
XLA Ops:
  0.0 1.2 %dynamic-slice_bitcast_fusion.2 = (bf16[1,128,512]{2,1,0:T(8,128)(2,1)S(1)}, bf16[1,128,512]{2,1,0:T(8,128)(2,1)S(1)}, bf16[1,128,512]{2,1,0:T(8,128)(2,1)S(1)}, bf16[1,128,512]{2,1,0:T(8,128)(2,1)S(1)}) fusion(bf16[128,1024]{1,0:T(8,128)(2,1)} %param.5, s32[]{:T(128)S(6)} %select_n.129, s32[]{:T(128)S(6)} %select_n.130, bf16[128,1024]{1,0:T(8,128)(2,1)} %param.4), kind=kLoop, calls=%fused_computation.4 | loop fusion | bytes 1048584 | tf_op jit(solution)/shard_map/stack | solution.py:159
  1.3 0.7 collective-permute-start.3
  2.0 0.8 constant_dynamic-slice_fusion.2
  2.8 0.2 collective-permute-start
  3.0 0.2 collective-permute-done.3
  3.3 0.1 collective-permute-start.9
  3.4 2.4 %collective-permute-start.12 = (bf16[2,256,256]{2,1,0:T(8,128)(2,1)S(1)}, bf16[2,256,256]{2,1,0:T(8,128)(2,1)S(1)}, u32[]{:S(2)}, u32[]{:S(2)}) collective-permute-start(bf16[2,256,256]{2,1,0:T(8,128)(2,1)S(1)} %get-tuple-element.29), channel_id=1, source_target_pairs={{0,6},{1,7},{2,4},{3,5},{4,2},{5,3},{6,0},{7,1},{8,14},{9,15},{10,... | collective-permute-start | bytes 786440 | tf_op jit(solution)/shard_map/ppermute | solution.py:19
  5.8 1.1 %collective-permute-start.6 = (bf16[2,256,256]{2,1,0:T(8,128)(2,1)S(1)}, bf16[2,256,256]{2,1,0:T(8,128)(2,1)S(1)}, u32[]{:S(2)}, u32[]{:S(2)}) collective-permute-start(bf16[2,256,256]{2,1,0:T(8,128)(2,1)S(1)} %get-tuple-element.29), channel_id=1, source_target_pairs={{0,2},{1,3},{2,0},{3,1},{4,6},{5,7},{6,4},{7,5},{8,10},{9,11},{10,... | collective-permute-start | bytes 786440 | tf_op jit(solution)/shard_map/ppermute | solution.py:19
  6.9 0.4 collective-permute-start.1
  7.3 0.3 collective-permute-start.4
  7.5 12.4 %collective-permute-done.9.refs_7_ = bf16[2,256,256]{2,1,0:T(8,128)(2,1)S(1)} collective-permute-done((bf16[2,256,256]{2,1,0:T(8,128)(2,1)S(1)}, bf16[2,256,256]{2,1,0:T(8,128)(2,1)S(1)}, u32[]{:S(2)}, u32[]{:S(2)}) %collective-permute-start.9) | collective-permute-done | bytes 262176 | tf_op jit(solution)/shard_map/ppermute | solution.py:19
  19.9 0.5 collective-permute-start.10
  20.4 8.9 %collective-permute-done.12.refs_8_ = bf16[2,256,256]{2,1,0:T(8,128)(2,1)S(1)} collective-permute-done((bf16[2,256,256]{2,1,0:T(8,128)(2,1)S(1)}, bf16[2,256,256]{2,1,0:T(8,128)(2,1)S(1)}, u32[]{:S(2)}, u32[]{:S(2)}) %collective-permute-start.12) | collective-permute-done | bytes 262176 | tf_op jit(solution)/shard_map/ppermute | solution.py:19
  29.4 0.3 collective-permute-start.13
  29.6 1.2 %collective-permute-start.7 = (bf16[2,256,256]{2,1,0:T(8,128)(2,1)S(1)}, bf16[2,256,256]{2,1,0:T(8,128)(2,1)S(1)}, u32[]{:S(2)}, u32[]{:S(2)}) collective-permute-start(bf16[2,256,256]{2,1,0:T(8,128)(2,1)S(1)} %collective-permute-done.6.refs_6_), channel_id=1, source_target_pairs={{0,8},{8,0},{16,24},{24,16},{1,9},{9,1},{17,25},{25,17},{2,10},{10... | collective-permute-start | bytes 786440 | tf_op jit(solution)/shard_map/ppermute | solution.py:19
  30.8 1.4 %collective-permute-start.2 = (bf16[128,1024]{1,0:T(8,128)(2,1)S(1)}, bf16[128,1024]{1,0:T(8,128)(2,1)S(1)}, u32[]{:S(2)}, u32[]{:S(2)}) collective-permute-start(bf16[128,1024]{1,0:T(8,128)(2,1)S(1)} %get-tuple-element.25), channel_id=1, source_target_pairs={{0,3},{1,2},{2,1},{3,0},{4,7},{5,6},{6,5},{7,4},{8,11},{9,10},{10,... | collective-permute-start | bytes 786440 | tf_op jit(solution)/shard_map/ppermute | solution.py:19
  32.2 1.3 %collective-permute-start.5 = (bf16[2,256,256]{2,1,0:T(8,128)(2,1)S(1)}, bf16[2,256,256]{2,1,0:T(8,128)(2,1)S(1)}, u32[]{:S(2)}, u32[]{:S(2)}) collective-permute-start(bf16[2,256,256]{2,1,0:T(8,128)(2,1)S(1)} %collective-permute-done.4.refs_5_), channel_id=1, source_target_pairs={{0,16},{24,8},{1,17},{25,9},{2,18},{26,10},{3,19},{27,11},{4,20},{... | collective-permute-start | bytes 786440 | tf_op jit(solution)/shard_map/ppermute | solution.py:29
  33.5 1.3 %collective-permute-start.11 = (bf16[2,256,256]{2,1,0:T(8,128)(2,1)S(1)}, bf16[2,256,256]{2,1,0:T(8,128)(2,1)S(1)}, u32[]{:S(2)}, u32[]{:S(2)}) collective-permute-start(bf16[2,256,256]{2,1,0:T(8,128)(2,1)S(1)} %collective-permute-done.10.refs_7_), channel_id=1, source_target_pairs={{0,16},{24,8},{1,17},{25,9},{2,18},{26,10},{3,19},{27,11},{4,20},{... | collective-permute-start | bytes 786440 | tf_op jit(solution)/shard_map/ppermute | solution.py:29
  34.8 1.9 %collective-permute-done.13.refs_8_ = bf16[2,256,256]{2,1,0:T(8,128)(2,1)S(1)} collective-permute-done((bf16[2,256,256]{2,1,0:T(8,128)(2,1)S(1)}, bf16[2,256,256]{2,1,0:T(8,128)(2,1)S(1)}, u32[]{:S(2)}, u32[]{:S(2)}) %collective-permute-start.13) | collective-permute-done | bytes 262176 | tf_op jit(solution)/shard_map/ppermute | solution.py:19
  36.7 1.3 %collective-permute-start.14 = (bf16[2,256,256]{2,1,0:T(8,128)(2,1)S(1)}, bf16[2,256,256]{2,1,0:T(8,128)(2,1)S(1)}, u32[]{:S(2)}, u32[]{:S(2)}) collective-permute-start(bf16[2,256,256]{2,1,0:T(8,128)(2,1)S(1)} %collective-permute-done.13.refs_8_), channel_id=1, source_target_pairs={{0,16},{24,8},{1,17},{25,9},{2,18},{26,10},{3,19},{27,11},{4,20},{... | collective-permute-start | bytes 786440 | tf_op jit(solution)/shard_map/ppermute | solution.py:29
  38.0 4.3 %collective-permute-done.7.refs_6_ = bf16[2,256,256]{2,1,0:T(8,128)(2,1)S(1)} collective-permute-done((bf16[2,256,256]{2,1,0:T(8,128)(2,1)S(1)}, bf16[2,256,256]{2,1,0:T(8,128)(2,1)S(1)}, u32[]{:S(2)}, u32[]{:S(2)}) %collective-permute-start.7) | collective-permute-done | bytes 262176 | tf_op jit(solution)/shard_map/ppermute | solution.py:19
  42.4 1.3 %collective-permute-start.8 = (bf16[2,256,256]{2,1,0:T(8,128)(2,1)S(1)}, bf16[2,256,256]{2,1,0:T(8,128)(2,1)S(1)}, u32[]{:S(2)}, u32[]{:S(2)}) collective-permute-start(bf16[2,256,256]{2,1,0:T(8,128)(2,1)S(1)} %collective-permute-done.7.refs_6_), channel_id=1, source_target_pairs={{0,16},{24,8},{1,17},{25,9},{2,18},{26,10},{3,19},{27,11},{4,20},{... | collective-permute-start | bytes 786440 | tf_op jit(solution)/shard_map/ppermute | solution.py:29
  43.7 6.5 %attend_first.1 = (f32[2,4,512,128]{3,2,1,0:T(8,128)S(1)}, f32[2,4,512,128]{3,2,1,0:T(8,128)S(1)}, f32[2,4,512,128]{3,2,1,0:T(8,128)S(1)}) custom-call(s32[1]{0:T(128)} %constant.132.clone.1.refs_0_, bf16[128,1024]{1,0:T(8,128)(2,1)S(1)} %get-tuple-element.27.refs_1_, bf16[128,1024]{1,0:T(8,128)(2,1)S(1)} %collective-permute-done.refs_2_, ...), custom_call_target="tpu_custom_call" | custom-call | flops 2147483648 | bytes 8388608 | tf_op jit(solution)/shard_map/attend_first/pallas_call | solution.py:132
  50.2 1.3 %copy-done = f32[2,4,512,128]{3,2,1,0:T(8,128)} copy-done((f32[2,4,512,128]{3,2,1,0:T(8,128)}, f32[2,4,512,128]{3,2,1,0:T(8,128)S(1)}, u32[]{:S(2)}) %copy-start) | copy-done | bytes 2097176
  51.5 9.3 %attend_next.1 = (f32[2,4,512,128]{3,2,1,0:T(8,128)S(1)}, f32[2,4,512,128]{3,2,1,0:T(8,128)S(1)}, f32[2,4,512,128]{3,2,1,0:T(8,128)S(1)}) custom-call(s32[1]{0:T(128)} %constant.132.clone.1.refs_0_, bf16[128,1024]{1,0:T(8,128)(2,1)S(1)} %get-tuple-element.27.refs_1_, bf16[128,1024]{1,0:T(8,128)(2,1)S(1)} %collective-permute-done.refs_2_, ...), custom_call_target="tpu_custom_call" | custom-call | flops 2147483648 | bytes 8388608 | tf_op jit(solution)/shard_map/attend_next/pallas_call | solution.py:132
  60.8 7.9 %attend_last.1 = (bf16[128,1024]{1,0:T(8,128)(2,1)S(1)}, bf16[128,1024]{1,0:T(8,128)(2,1)S(1)}, bf16[128,1024]{1,0:T(8,128)(2,1)S(1)}, bf16[128,1024]{1,0:T(8,128)(2,1)S(1)}) custom-call(s32[1]{0:T(128)} %bitcast.refs_0_, bf16[128,1024]{1,0:T(8,128)(2,1)S(1)} %get-tuple-element.27.refs_1_, bf16[128,1024]{1,0:T(8,128)(2,1)S(1)} %collective-permute-done.refs_2_, ...), custom_call_target="tpu_custom_call" | custom-call | flops 2147483648 | bytes 8388608 | tf_op jit(solution)/shard_map/attend_last/pallas_call | solution.py:132
  68.7 1.4 %collective-permute-start.15 = (bf16[128,1024]{1,0:T(8,128)(2,1)S(1)}, bf16[128,1024]{1,0:T(8,128)(2,1)S(1)}, u32[]{:S(2)}, u32[]{:S(2)}) collective-permute-start(bf16[128,1024]{1,0:T(8,128)(2,1)S(1)} %get-tuple-element.22), channel_id=1, source_target_pairs={{0,1},{1,0},{2,3},{3,2},{4,5},{5,4},{6,7},{7,6},{8,9},{9,8},{10,11... | collective-permute-start | bytes 786440 | tf_op jit(solution)/shard_map/ppermute | solution.py:19
  70.1 1.2 %collective-permute-start.16 = (bf16[128,1024]{1,0:T(8,128)(2,1)S(1)}, bf16[128,1024]{1,0:T(8,128)(2,1)S(1)}, u32[]{:S(2)}, u32[]{:S(2)}) collective-permute-start(bf16[128,1024]{1,0:T(8,128)(2,1)S(1)} %get-tuple-element.23), channel_id=1, source_target_pairs={{0,2},{1,3},{2,0},{3,1},{4,6},{5,7},{6,4},{7,5},{8,10},{9,11},{10,... | collective-permute-start | bytes 786440 | tf_op jit(solution)/shard_map/ppermute | solution.py:19
  71.3 0.5 collective-permute-start.17
  72.0 5.9 %collective-permute-done.16 = bf16[128,1024]{1,0:T(8,128)(2,1)S(1)} collective-permute-done((bf16[128,1024]{1,0:T(8,128)(2,1)S(1)}, bf16[128,1024]{1,0:T(8,128)(2,1)S(1)}, u32[]{:S(2)}, u32[]{:S(2)}) %collective-permute-start.16) | collective-permute-done | bytes 262176 | tf_op jit(solution)/shard_map/ppermute | solution.py:19
  77.9 5.8 %collective-permute-done.17 = bf16[128,1024]{1,0:T(8,128)(2,1)S(1)} collective-permute-done((bf16[128,1024]{1,0:T(8,128)(2,1)S(1)}, bf16[128,1024]{1,0:T(8,128)(2,1)S(1)}, u32[]{:S(2)}, u32[]{:S(2)}) %collective-permute-start.17) | collective-permute-done | bytes 262176 | tf_op jit(solution)/shard_map/ppermute | solution.py:19
  83.8 0.7 constant_dynamic-update-slice_fusion
  (23 shorter events, 0.3 us)
Async XLA Ops:
  0.0 2.0 %copy-start.1 = (bf16[128,4096]{1,0:T(8,128)(2,1)S(1)}, bf16[128,4096]{1,0:T(8,128)(2,1)}, u32[]{:S(2)}) copy-start(bf16[128,4096]{1,0:T(8,128)(2,1)} %param.3) | copy-start | bytes 3145732
  1.3 1.9 %collective-permute-start.3 = (bf16[2,128,512]{2,1,0:T(8,128)(2,1)S(1)}, bf16[2,128,512]{2,1,0:T(8,128)(2,1)S(1)}, u32[]{:S(2)}, u32[]{:S(2)}) collective-permute-start(bf16[2,128,512]{2,1,0:T(8,128)(2,1)S(1)} %pad_maximum_fusion.1), channel_id=1, source_target_pairs={{0,1},{1,0},{2,3},{3,2},{4,5},{5,4},{6,7},{7,6},{8,9},{9,8},{10,11... | collective-permute-start | bytes 786440 | tf_op jit(solution)/shard_map/ppermute | solution.py:19
  2.8 4.5 %collective-permute-start = (bf16[128,1024]{1,0:T(8,128)(2,1)S(1)}, bf16[128,1024]{1,0:T(8,128)(2,1)S(1)}, u32[]{:S(2)}, u32[]{:S(2)}) collective-permute-start(bf16[128,1024]{1,0:T(8,128)(2,1)S(1)} %get-tuple-element.26), channel_id=1, source_target_pairs={{0,1},{1,0},{2,3},{3,2},{4,5},{5,4},{6,7},{7,6},{8,9},{9,8},{10,11... | collective-permute-start | bytes 786440 | tf_op jit(solution)/shard_map/ppermute | solution.py:19
  3.3 16.7 %collective-permute-start.9 = (bf16[2,256,256]{2,1,0:T(8,128)(2,1)S(1)}, bf16[2,256,256]{2,1,0:T(8,128)(2,1)S(1)}, u32[]{:S(2)}, u32[]{:S(2)}) collective-permute-start(bf16[2,256,256]{2,1,0:T(8,128)(2,1)S(1)} %get-tuple-element.30.refs_5_), channel_id=1, source_target_pairs={{0,4},{1,5},{2,6},{3,7},{4,0},{5,1},{6,2},{7,3},{8,12},{9,13},{10,... | collective-permute-start | bytes 786440 | tf_op jit(solution)/shard_map/ppermute | solution.py:19
  3.4 26.0 %collective-permute-start.12 = (bf16[2,256,256]{2,1,0:T(8,128)(2,1)S(1)}, bf16[2,256,256]{2,1,0:T(8,128)(2,1)S(1)}, u32[]{:S(2)}, u32[]{:S(2)}) collective-permute-start(bf16[2,256,256]{2,1,0:T(8,128)(2,1)S(1)} %get-tuple-element.29), channel_id=1, source_target_pairs={{0,6},{1,7},{2,4},{3,5},{4,2},{5,3},{6,0},{7,1},{8,14},{9,15},{10,... | collective-permute-start | bytes 786440 | tf_op jit(solution)/shard_map/ppermute | solution.py:19
  5.8 23.8 %collective-permute-start.6 = (bf16[2,256,256]{2,1,0:T(8,128)(2,1)S(1)}, bf16[2,256,256]{2,1,0:T(8,128)(2,1)S(1)}, u32[]{:S(2)}, u32[]{:S(2)}) collective-permute-start(bf16[2,256,256]{2,1,0:T(8,128)(2,1)S(1)} %get-tuple-element.29), channel_id=1, source_target_pairs={{0,2},{1,3},{2,0},{3,1},{4,6},{5,7},{6,4},{7,5},{8,10},{9,11},{10,... | collective-permute-start | bytes 786440 | tf_op jit(solution)/shard_map/ppermute | solution.py:19
  6.9 24.0 %collective-permute-start.1 = (bf16[128,1024]{1,0:T(8,128)(2,1)}, bf16[128,1024]{1,0:T(8,128)(2,1)S(1)}, u32[]{:S(2)}, u32[]{:S(2)}) collective-permute-start(bf16[128,1024]{1,0:T(8,128)(2,1)} %get-tuple-element.28), channel_id=1, source_target_pairs={{0,2},{1,3},{2,0},{3,1},{4,6},{5,7},{6,4},{7,5},{8,10},{9,11},{10,... | collective-permute-start | bytes 786440 | tf_op jit(solution)/shard_map/ppermute | solution.py:19
  7.3 25.0 %collective-permute-start.4 = (bf16[2,256,256]{2,1,0:T(8,128)(2,1)S(1)}, bf16[2,256,256]{2,1,0:T(8,128)(2,1)S(1)}, u32[]{:S(2)}, u32[]{:S(2)}) collective-permute-start(bf16[2,256,256]{2,1,0:T(8,128)(2,1)S(1)} %get-tuple-element.30.refs_5_), channel_id=1, source_target_pairs={{0,8},{8,0},{16,24},{24,16},{1,9},{9,1},{17,25},{25,17},{2,10},{10... | collective-permute-start | bytes 786440 | tf_op jit(solution)/shard_map/ppermute | solution.py:19
  19.9 13.6 %collective-permute-start.10 = (bf16[2,256,256]{2,1,0:T(8,128)(2,1)S(1)}, bf16[2,256,256]{2,1,0:T(8,128)(2,1)S(1)}, u32[]{:S(2)}, u32[]{:S(2)}) collective-permute-start(bf16[2,256,256]{2,1,0:T(8,128)(2,1)S(1)} %collective-permute-done.9.refs_7_), channel_id=1, source_target_pairs={{0,8},{8,0},{16,24},{24,16},{1,9},{9,1},{17,25},{25,17},{2,10},{10... | collective-permute-start | bytes 786440 | tf_op jit(solution)/shard_map/ppermute | solution.py:19
  29.4 7.4 %collective-permute-start.13 = (bf16[2,256,256]{2,1,0:T(8,128)(2,1)S(1)}, bf16[2,256,256]{2,1,0:T(8,128)(2,1)S(1)}, u32[]{:S(2)}, u32[]{:S(2)}) collective-permute-start(bf16[2,256,256]{2,1,0:T(8,128)(2,1)S(1)} %collective-permute-done.12.refs_8_), channel_id=1, source_target_pairs={{0,8},{8,0},{16,24},{24,16},{1,9},{9,1},{17,25},{25,17},{2,10},{10... | collective-permute-start | bytes 786440 | tf_op jit(solution)/shard_map/ppermute | solution.py:19
  29.6 12.7 %collective-permute-start.7 = (bf16[2,256,256]{2,1,0:T(8,128)(2,1)S(1)}, bf16[2,256,256]{2,1,0:T(8,128)(2,1)S(1)}, u32[]{:S(2)}, u32[]{:S(2)}) collective-permute-start(bf16[2,256,256]{2,1,0:T(8,128)(2,1)S(1)} %collective-permute-done.6.refs_6_), channel_id=1, source_target_pairs={{0,8},{8,0},{16,24},{24,16},{1,9},{9,1},{17,25},{25,17},{2,10},{10... | collective-permute-start | bytes 786440 | tf_op jit(solution)/shard_map/ppermute | solution.py:19
  30.8 12.8 %collective-permute-start.2 = (bf16[128,1024]{1,0:T(8,128)(2,1)S(1)}, bf16[128,1024]{1,0:T(8,128)(2,1)S(1)}, u32[]{:S(2)}, u32[]{:S(2)}) collective-permute-start(bf16[128,1024]{1,0:T(8,128)(2,1)S(1)} %get-tuple-element.25), channel_id=1, source_target_pairs={{0,3},{1,2},{2,1},{3,0},{4,7},{5,6},{6,5},{7,4},{8,11},{9,10},{10,... | collective-permute-start | bytes 786440 | tf_op jit(solution)/shard_map/ppermute | solution.py:19
  32.2 28.5 %collective-permute-start.5 = (bf16[2,256,256]{2,1,0:T(8,128)(2,1)S(1)}, bf16[2,256,256]{2,1,0:T(8,128)(2,1)S(1)}, u32[]{:S(2)}, u32[]{:S(2)}) collective-permute-start(bf16[2,256,256]{2,1,0:T(8,128)(2,1)S(1)} %collective-permute-done.4.refs_5_), channel_id=1, source_target_pairs={{0,16},{24,8},{1,17},{25,9},{2,18},{26,10},{3,19},{27,11},{4,20},{... | collective-permute-start | bytes 786440 | tf_op jit(solution)/shard_map/ppermute | solution.py:29
  33.5 27.2 %collective-permute-start.11 = (bf16[2,256,256]{2,1,0:T(8,128)(2,1)S(1)}, bf16[2,256,256]{2,1,0:T(8,128)(2,1)S(1)}, u32[]{:S(2)}, u32[]{:S(2)}) collective-permute-start(bf16[2,256,256]{2,1,0:T(8,128)(2,1)S(1)} %collective-permute-done.10.refs_7_), channel_id=1, source_target_pairs={{0,16},{24,8},{1,17},{25,9},{2,18},{26,10},{3,19},{27,11},{4,20},{... | collective-permute-start | bytes 786440 | tf_op jit(solution)/shard_map/ppermute | solution.py:29
  36.7 24.0 %collective-permute-start.14 = (bf16[2,256,256]{2,1,0:T(8,128)(2,1)S(1)}, bf16[2,256,256]{2,1,0:T(8,128)(2,1)S(1)}, u32[]{:S(2)}, u32[]{:S(2)}) collective-permute-start(bf16[2,256,256]{2,1,0:T(8,128)(2,1)S(1)} %collective-permute-done.13.refs_8_), channel_id=1, source_target_pairs={{0,16},{24,8},{1,17},{25,9},{2,18},{26,10},{3,19},{27,11},{4,20},{... | collective-permute-start | bytes 786440 | tf_op jit(solution)/shard_map/ppermute | solution.py:29
  42.4 18.4 %collective-permute-start.8 = (bf16[2,256,256]{2,1,0:T(8,128)(2,1)S(1)}, bf16[2,256,256]{2,1,0:T(8,128)(2,1)S(1)}, u32[]{:S(2)}, u32[]{:S(2)}) collective-permute-start(bf16[2,256,256]{2,1,0:T(8,128)(2,1)S(1)} %collective-permute-done.7.refs_6_), channel_id=1, source_target_pairs={{0,16},{24,8},{1,17},{25,9},{2,18},{26,10},{3,19},{27,11},{4,20},{... | collective-permute-start | bytes 786440 | tf_op jit(solution)/shard_map/ppermute | solution.py:29
  50.2 1.3 %copy-start = (f32[2,4,512,128]{3,2,1,0:T(8,128)}, f32[2,4,512,128]{3,2,1,0:T(8,128)S(1)}, u32[]{:S(2)}) copy-start(f32[2,4,512,128]{3,2,1,0:T(8,128)S(1)} %get-tuple-element.17.refs_11_) | copy-start | bytes 6291460
  68.7 3.3 %collective-permute-start.15 = (bf16[128,1024]{1,0:T(8,128)(2,1)S(1)}, bf16[128,1024]{1,0:T(8,128)(2,1)S(1)}, u32[]{:S(2)}, u32[]{:S(2)}) collective-permute-start(bf16[128,1024]{1,0:T(8,128)(2,1)S(1)} %get-tuple-element.22), channel_id=1, source_target_pairs={{0,1},{1,0},{2,3},{3,2},{4,5},{5,4},{6,7},{7,6},{8,9},{9,8},{10,11... | collective-permute-start | bytes 786440 | tf_op jit(solution)/shard_map/ppermute | solution.py:19
  70.1 7.8 %collective-permute-start.16 = (bf16[128,1024]{1,0:T(8,128)(2,1)S(1)}, bf16[128,1024]{1,0:T(8,128)(2,1)S(1)}, u32[]{:S(2)}, u32[]{:S(2)}) collective-permute-start(bf16[128,1024]{1,0:T(8,128)(2,1)S(1)} %get-tuple-element.23), channel_id=1, source_target_pairs={{0,2},{1,3},{2,0},{3,1},{4,6},{5,7},{6,4},{7,5},{8,10},{9,11},{10,... | collective-permute-start | bytes 786440 | tf_op jit(solution)/shard_map/ppermute | solution.py:19
  71.3 12.5 %collective-permute-start.17 = (bf16[128,1024]{1,0:T(8,128)(2,1)S(1)}, bf16[128,1024]{1,0:T(8,128)(2,1)S(1)}, u32[]{:S(2)}, u32[]{:S(2)}) collective-permute-start(bf16[128,1024]{1,0:T(8,128)(2,1)S(1)} %get-tuple-element.24), channel_id=1, source_target_pairs={{0,3},{1,2},{2,1},{3,0},{4,7},{5,6},{6,5},{7,4},{8,11},{9,10},{10,... | collective-permute-start | bytes 786440 | tf_op jit(solution)/shard_map/ppermute | solution.py:19
  77.9 5.8 %copy-start.2 = (bf16[128,4096]{1,0:T(8,128)(2,1)}, bf16[128,4096]{1,0:T(8,128)(2,1)S(1)}, u32[]{:S(2)}) copy-start(bf16[128,4096]{1,0:T(8,128)(2,1)S(1)} %constant_dynamic-update-slice_fusion.1) | copy-start | bytes 3145732
